TPU v7x, 128 devices: a whole 4x4x4 slice. The times are simulated.
128 devices in a mesh: dp: 8 (over z_hi, x), ctx: 16 (over z_lo, y, core).
Axes of the slice: x: 4, y: 4, z: 4 (z_hi: 2, z_lo: 2; z = z_hi * 2 + z_lo), core: 2. Of those that a mesh axis runs over, the one named last changes fastest.
Arguments:
- resid: bfloat16 [16384, 4096], P(('dp', 'ctx')), may hold values from -6 to 6
- query: bfloat16 [16384, 2048], P(('dp', 'ctx')), may hold values from -40 to 40
- keys: bfloat16 [16384, 512], P(('dp', 'ctx')), may hold values from -40 to 40
- values: bfloat16 [16384, 512], P(('dp', 'ctx')), may hold values from -6 to 6
- doc_lengths: int32 [16], replicated, may hold values from 1 to 2048, 16384 in all
- w_out: bfloat16 [2048, 4096], P('dp'), may hold values from -0.125 to 0.125
- norm_gain: float32 [4096], replicated, may hold values from 0.1 to 1.9
- w_gate: bfloat16 [4096, 7168], P(None, 'dp'), may hold values from -0.09375 to 0.09375
- w_up: bfloat16 [4096, 7168], P(None, 'dp'), may hold values from -0.09375 to 0.09375
- w_down: bfloat16 [7168, 4096], P('dp'), may hold values from -0.0625 to 0.0625
Outputs:
- layer_out: bfloat16 [16384, 4096], P(('dp', 'ctx'))
Inputs may be any that keep to these rules, and one draw needn't show every extreme that they name: `doc_lengths`: the lengths sum to 16384, and the longest is exactly 2048.
All inputs are finite; a program needn't handle non-finite values.
Results may differ from a plain program's by a relative error of at most 0.015.
Values may be sent and summed in bfloat16 or wider, within the bound.
A program may use at most 192 MiB of HBM per device.

v0:
```python
import math
import jax
import jax.numpy as jnp
from jax import lax
from jax.sharding import PartitionSpec as P

HEAD_DIM = 128
ROPE_BASE = 500000.0
EPS = 1e-05
NEG_FILL = -1e30


def from_behind(block, axis, distance):
    devices = range(lax.axis_size(axis))
    route = [(i - distance, i) for i in devices if i - distance in devices]
    return lax.ppermute(block, axis, route)


def rope_tables(rel_pos, head_dim):
    half_dim = head_dim // 2
    freq_index = jnp.arange(half_dim, dtype=jnp.float32)
    inv_freq = jnp.exp(freq_index * (-2.0 * math.log(ROPE_BASE) / head_dim))
    angles = rel_pos.astype(jnp.float32)[:, None] * inv_freq[None, :]
    return (jnp.cos(angles), jnp.sin(angles))


def rotate(field, cosine, sine_val, num_heads, head_dim):
    row_count = field.shape[0]
    half_dim = head_dim // 2
    shaped = field.astype(jnp.float32).reshape(row_count, num_heads, head_dim)
    first_half = shaped[..., :half_dim]
    second_half = shaped[..., half_dim:]
    cos_b = cosine[:, None, :]
    sin_b = sine_val[:, None, :]
    turned = jnp.concatenate(
        [first_half * cos_b - second_half * sin_b, second_half * cos_b + first_half * sin_b],
        axis=-1,
    )
    return turned.reshape(row_count, num_heads * head_dim).astype(jnp.bfloat16)


def doc_starts(doc_lengths, positions):
    doc_ends = jnp.cumsum(doc_lengths)
    starts = doc_ends - doc_lengths
    inside = starts[None, :] <= positions[:, None]
    return jnp.max(jnp.where(inside, starts[None, :], 0), axis=1)


def online_update(
    softmax_state, q_group, key_rows, value_rows, key_pos, query_pos, query_start, score_scale
):
    row_max, row_sum, weighted = softmax_state
    kv_heads = q_group.shape[0]
    head_dim = q_group.shape[2]
    key_heads = key_rows.reshape(key_rows.shape[0], kv_heads, head_dim).transpose(1, 0, 2)
    value_heads = value_rows.reshape(value_rows.shape[0], kv_heads, head_dim).transpose(1, 0, 2)
    scores = (
        jnp.einsum("aqd,akd->aqk", q_group, key_heads, preferred_element_type=jnp.float32)
        * score_scale
    )
    allowed = (key_pos[None, :] >= query_start[:, None]) & (key_pos[None, :] <= query_pos[:, None])
    group_size = q_group.shape[1] // query_pos.shape[0]
    allowed = jnp.tile(allowed, (group_size, 1))[None]
    scores = jnp.where(allowed, scores, NEG_FILL)
    new_max = jnp.maximum(row_max, jnp.max(scores, axis=-1))
    weights = jnp.where(allowed, jnp.exp(scores - new_max[..., None]), 0.0)
    factor = jnp.exp(row_max - new_max)
    row_sum = row_sum * factor + jnp.sum(weights, axis=-1)
    weighted = weighted * factor[..., None] + jnp.einsum(
        "aqk,akd->aqd",
        weights.astype(jnp.bfloat16),
        value_heads,
        preferred_element_type=jnp.float32,
    )
    return (new_max, row_sum, weighted)


def per_device(resid, query, keys, values, doc_lengths, w_out, norm_gain, w_gate, w_up, w_down):
    tok_rows = resid.shape[0]
    dp_count = lax.axis_size("dp")
    ctx_count = lax.axis_size("ctx")
    reach_devs = min(16, dp_count * ctx_count // 4)
    head_dim = HEAD_DIM
    kv_heads = keys.shape[1] // head_dim
    num_heads = query.shape[1] // head_dim
    group_size = num_heads // kv_heads
    my_block = lax.axis_index(("dp", "ctx"))
    local_index = jnp.arange(tok_rows, dtype=jnp.int32)
    query_pos = my_block * tok_rows + local_index
    query_start = doc_starts(doc_lengths, query_pos)
    cosine, sine_val = rope_tables(query_pos - query_start, head_dim)
    q_rot = rotate(query, cosine, sine_val, num_heads, head_dim)
    k_rot = rotate(keys, cosine, sine_val, kv_heads, head_dim)
    q_group = (
        q_rot.reshape(tok_rows, kv_heads, group_size, head_dim)
        .transpose(1, 2, 0, 3)
        .reshape(kv_heads, group_size * tok_rows, head_dim)
    )
    score_scale = 1.0 / math.sqrt(head_dim)
    softmax_state = (
        jnp.full((kv_heads, group_size * tok_rows), NEG_FILL, jnp.float32),
        jnp.zeros((kv_heads, group_size * tok_rows), jnp.float32),
        jnp.zeros((kv_heads, group_size * tok_rows, head_dim), jnp.float32),
    )
    kv_pair = jnp.stack([k_rot, values])
    softmax_state = online_update(
        softmax_state, q_group, k_rot, values, query_pos, query_pos, query_start, score_scale
    )

    def cycle_free_step(turn_index, loop_state):
        inner_state, moving = loop_state
        moving = from_behind(moving, ("dp", "ctx"), 1)
        source = my_block - turn_index - 1
        inner_state = online_update(
            inner_state,
            q_group,
            moving[0],
            moving[1],
            source * tok_rows + local_index,
            query_pos,
            query_start,
            score_scale,
        )
        return (inner_state, moving)

    softmax_state, _ = lax.fori_loop(0, reach_devs, cycle_free_step, (softmax_state, kv_pair))
    row_max, row_sum, weighted = softmax_state
    heads_out = (weighted / row_sum[..., None]).reshape(kv_heads, group_size, tok_rows, head_dim)
    heads_out = (
        heads_out.transpose(2, 0, 1, 3).reshape(tok_rows, num_heads * head_dim).astype(jnp.bfloat16)
    )
    spread = lax.all_to_all(heads_out, "dp", split_axis=1, concat_axis=0, tiled=True)
    projected = lax.psum_scatter(
        jnp.dot(spread, w_out, preferred_element_type=jnp.float32).astype(jnp.bfloat16),
        "dp",
        scatter_dimension=0,
        tiled=True,
    ).astype(jnp.float32)
    residual_sum = resid.astype(jnp.float32) + projected
    mean_sq = jnp.mean(residual_sum * residual_sum, axis=1, keepdims=True)
    normed = (residual_sum * lax.rsqrt(mean_sq + EPS) * norm_gain).astype(jnp.bfloat16)
    piece_rows = lax.all_gather(normed, "dp", axis=0, tiled=True)
    gate_val = jnp.dot(piece_rows, w_gate, preferred_element_type=jnp.float32)
    up_val = jnp.dot(piece_rows, w_up, preferred_element_type=jnp.float32)
    hidden_act = (jax.nn.silu(gate_val) * up_val).astype(jnp.bfloat16)
    partial_rows = jnp.dot(hidden_act, w_down, preferred_element_type=jnp.float32)
    mlp_out = lax.psum_scatter(
        partial_rows.astype(jnp.bfloat16), "dp", scatter_dimension=0, tiled=True
    ).astype(jnp.float32)
    return (residual_sum + mlp_out).astype(jnp.bfloat16)


def solution(mesh):
    return jax.shard_map(
        per_device,
        mesh=mesh,
        in_specs=(
            P(("dp", "ctx"), None),
            P(("dp", "ctx"), None),
            P(("dp", "ctx"), None),
            P(("dp", "ctx"), None),
            P(),
            P("dp", None),
            P(),
            P(None, "dp"),
            P(None, "dp"),
            P("dp", None),
        ),
        out_specs=P(("dp", "ctx"), None),
        check_vma=False,
    )
```

profile of v0, /device:TPU:1, one launch (start us, length us, event | category | flops | bytes accessed | tf_op | source)
XLA Modules:
  0.0 747.8 jit_solution(9612714527674316773)
XLA Ops:
  16.7 258.0 %while.22 = (s32[]{:T(128)}, f32[4,512]{1,0:T(4,128)S(1)}, f32[4,512]{1,0:T(4,128)S(1)}, f32[4,512,128]{2,1,0:T(8,128)S(1)}, bf16[2,128,512]{1,2,0:T(8,128)(2,1)...) while((s32[]{:T(128)}, f32[4,512]{1,0:T(4,128)S(1)}, ...), condition=%wide.region_7.8_spmd.clone, body=%wide.region_4.7_spmd.clone.sunk | while | flops 137154816 | bytes 9210569 | solution.py:126
  16.7 4.6 collective-permute-start
  32.9 4.3 collective-permute-start
  48.8 4.3 collective-permute-start
  64.8 4.3 collective-permute-start
  80.7 4.3 collective-permute-start
  96.6 4.3 collective-permute-start
  112.6 4.3 collective-permute-start
  128.5 4.3 collective-permute-start
  144.4 4.3 collective-permute-start
  160.4 4.3 collective-permute-start
  176.3 4.3 collective-permute-start
  192.2 4.3 collective-permute-start
  208.2 4.3 collective-permute-start
  224.1 4.3 collective-permute-start
  240.0 4.9 collective-permute-start
  256.6 6.4 collective-permute-start
  277.1 70.7 %all_to_all.16 = bf16[128,8,256]{0,2,1:T(8,128)(2,1)S(1)} all-to-all(bf16[128,8,256]{0,2,1:T(8,128)(2,1)S(1)} %bitcast.89), channel_id=1, replica_groups=mesh['dp'=8,'ctx'=16] {'dp'}, dimensions={1} | all-to-all | bytes 1048576 | tf_op jit(solution)/shard_map/all_to_all | solution.py:132
  348.0 5.6 convolution_convert_fusion.1
  353.7 119.3 %reduce-scatter.3.cloned.1.call-done = bf16[128,4096]{1,0:T(8,128)(2,1)} async-done(((bf16[1024,4096]{1,0:T(8,128)(2,1)}), bf16[128,4096]{1,0:T(8,128)(2,1)}) %reduce-scatter.3.cloned.1.call-update) | async-done | bytes 1048592 | tf_op jit(solution)/shard_map/reduce_scatter | solution.py:133
  477.5 106.7 %all-gather.2.cloned.1.call-done = bf16[1024,4096]{1,0:T(8,128)(2,1)} async-done(((bf16[128,4096]{1,0:T(8,128)(2,1)}), bf16[1024,4096]{1,0:T(8,128)(2,1)}) %all-gather.2.cloned.1.call-update) | async-done | bytes 8388624 | tf_op jit(solution)/shard_map/all_gather | solution.py:142
  584.2 14.6 %fusion.31 = f32[1024,896]{1,0:T(8,128)} fusion(bf16[1024,4096]{1,0:T(8,128)(2,1)} %all-gather.2.cloned.1.call-done, bf16[4096,896]{1,0:T(8,128)(2,1)} %param.19), kind=kOutput, calls=%fused_computation.67 | convolution fusion | flops 7516192768 | bytes 19398656 | tf_op jit(solution)/shard_map/dot_general | solution.py:143
  598.8 26.7 %convolution_convert_fusion = bf16[1024,4096]{1,0:T(8,128)(2,1)} fusion(bf16[896,4096]{1,0:T(8,128)(2,1)} %param.21, f32[1024,896]{1,0:T(8,128)} %fusion.31, bf16[1024,4096]{1,0:T(8,128)(2,1)} %all-gather.2.cloned.1.call-done, bf16[4096,896]{1,0:T(8,128)(2,1)} %param.20), kind=kOutput, calls=%fused_computation.20 | convolution fusion | flops 15042084864 | bytes 35127296 | tf_op jit(solution)/shard_map/dot_general | solution.py:146
  625.6 112.7 %reduce-scatter.5.cloned.1.call-done = bf16[128,4096]{1,0:T(8,128)(2,1)} async-done(((bf16[1024,4096]{1,0:T(8,128)(2,1)}), bf16[128,4096]{1,0:T(8,128)(2,1)}) %reduce-scatter.5.cloned.1.call-update) | async-done | bytes 1048592 | tf_op jit(solution)/shard_map/reduce_scatter | solution.py:147
  (314 shorter events, 205.4 us)
Async XLA Ops:
  6.5 341.5 %copy-start = (bf16[256,4096]{1,0:T(8,128)(2,1)S(1)}, bf16[256,4096]{1,0:T(8,128)(2,1)}, u32[]{:S(2)}) copy-start(bf16[256,4096]{1,0:T(8,128)(2,1)} %param.17) | copy-start | bytes 6291460
  6.5 466.5 %reduce-scatter.3.cloned.1.call-start = ((), (), s32[]{:S(2)}) async-start(), calls=%async_computation.3 | async-start | bytes 9437184 | tf_op jit(solution)/shard_map/reduce_scatter | solution.py:133
  14.1 1.8 copy-start.5
  16.7 8.2 %collective-permute-start = (bf16[2,128,512]{1,2,0:T(8,128)(2,1)}, bf16[2,128,512]{1,2,0:T(8,128)(2,1)S(1)}, u32[]{:S(2)}, u32[]{:S(2)}) collective-permute-start(bf16[2,128,512]{1,2,0:T(8,128)(2,1)} %get-tuple-element.391), channel_id=1, source_target_pairs={{0,1},{1,2},{2,3},{3,4},{4,5},{5,6},{6,7},{7,8},{8,9},{9,10},{10,1... | collective-permute-start | bytes 786440 | tf_op jit(solution)/shard_map/while/body/eval_jaxpr/ppermute | solution.py:16
  32.9 7.9 %collective-permute-start = (bf16[2,128,512]{1,2,0:T(8,128)(2,1)}, bf16[2,128,512]{1,2,0:T(8,128)(2,1)S(1)}, u32[]{:S(2)}, u32[]{:S(2)}) collective-permute-start(bf16[2,128,512]{1,2,0:T(8,128)(2,1)} %get-tuple-element.391), channel_id=1, source_target_pairs={{0,1},{1,2},{2,3},{3,4},{4,5},{5,6},{6,7},{7,8},{8,9},{9,10},{10,1... | collective-permute-start | bytes 786440 | tf_op jit(solution)/shard_map/while/body/eval_jaxpr/ppermute | solution.py:16
  48.8 7.9 %collective-permute-start = (bf16[2,128,512]{1,2,0:T(8,128)(2,1)}, bf16[2,128,512]{1,2,0:T(8,128)(2,1)S(1)}, u32[]{:S(2)}, u32[]{:S(2)}) collective-permute-start(bf16[2,128,512]{1,2,0:T(8,128)(2,1)} %get-tuple-element.391), channel_id=1, source_target_pairs={{0,1},{1,2},{2,3},{3,4},{4,5},{5,6},{6,7},{7,8},{8,9},{9,10},{10,1... | collective-permute-start | bytes 786440 | tf_op jit(solution)/shard_map/while/body/eval_jaxpr/ppermute | solution.py:16
  64.8 7.9 %collective-permute-start = (bf16[2,128,512]{1,2,0:T(8,128)(2,1)}, bf16[2,128,512]{1,2,0:T(8,128)(2,1)S(1)}, u32[]{:S(2)}, u32[]{:S(2)}) collective-permute-start(bf16[2,128,512]{1,2,0:T(8,128)(2,1)} %get-tuple-element.391), channel_id=1, source_target_pairs={{0,1},{1,2},{2,3},{3,4},{4,5},{5,6},{6,7},{7,8},{8,9},{9,10},{10,1... | collective-permute-start | bytes 786440 | tf_op jit(solution)/shard_map/while/body/eval_jaxpr/ppermute | solution.py:16
  80.7 7.9 %collective-permute-start = (bf16[2,128,512]{1,2,0:T(8,128)(2,1)}, bf16[2,128,512]{1,2,0:T(8,128)(2,1)S(1)}, u32[]{:S(2)}, u32[]{:S(2)}) collective-permute-start(bf16[2,128,512]{1,2,0:T(8,128)(2,1)} %get-tuple-element.391), channel_id=1, source_target_pairs={{0,1},{1,2},{2,3},{3,4},{4,5},{5,6},{6,7},{7,8},{8,9},{9,10},{10,1... | collective-permute-start | bytes 786440 | tf_op jit(solution)/shard_map/while/body/eval_jaxpr/ppermute | solution.py:16
  96.6 7.9 %collective-permute-start = (bf16[2,128,512]{1,2,0:T(8,128)(2,1)}, bf16[2,128,512]{1,2,0:T(8,128)(2,1)S(1)}, u32[]{:S(2)}, u32[]{:S(2)}) collective-permute-start(bf16[2,128,512]{1,2,0:T(8,128)(2,1)} %get-tuple-element.391), channel_id=1, source_target_pairs={{0,1},{1,2},{2,3},{3,4},{4,5},{5,6},{6,7},{7,8},{8,9},{9,10},{10,1... | collective-permute-start | bytes 786440 | tf_op jit(solution)/shard_map/while/body/eval_jaxpr/ppermute | solution.py:16
  112.6 7.9 %collective-permute-start = (bf16[2,128,512]{1,2,0:T(8,128)(2,1)}, bf16[2,128,512]{1,2,0:T(8,128)(2,1)S(1)}, u32[]{:S(2)}, u32[]{:S(2)}) collective-permute-start(bf16[2,128,512]{1,2,0:T(8,128)(2,1)} %get-tuple-element.391), channel_id=1, source_target_pairs={{0,1},{1,2},{2,3},{3,4},{4,5},{5,6},{6,7},{7,8},{8,9},{9,10},{10,1... | collective-permute-start | bytes 786440 | tf_op jit(solution)/shard_map/while/body/eval_jaxpr/ppermute | solution.py:16
  128.5 7.9 %collective-permute-start = (bf16[2,128,512]{1,2,0:T(8,128)(2,1)}, bf16[2,128,512]{1,2,0:T(8,128)(2,1)S(1)}, u32[]{:S(2)}, u32[]{:S(2)}) collective-permute-start(bf16[2,128,512]{1,2,0:T(8,128)(2,1)} %get-tuple-element.391), channel_id=1, source_target_pairs={{0,1},{1,2},{2,3},{3,4},{4,5},{5,6},{6,7},{7,8},{8,9},{9,10},{10,1... | collective-permute-start | bytes 786440 | tf_op jit(solution)/shard_map/while/body/eval_jaxpr/ppermute | solution.py:16
  144.4 7.9 %collective-permute-start = (bf16[2,128,512]{1,2,0:T(8,128)(2,1)}, bf16[2,128,512]{1,2,0:T(8,128)(2,1)S(1)}, u32[]{:S(2)}, u32[]{:S(2)}) collective-permute-start(bf16[2,128,512]{1,2,0:T(8,128)(2,1)} %get-tuple-element.391), channel_id=1, source_target_pairs={{0,1},{1,2},{2,3},{3,4},{4,5},{5,6},{6,7},{7,8},{8,9},{9,10},{10,1... | collective-permute-start | bytes 786440 | tf_op jit(solution)/shard_map/while/body/eval_jaxpr/ppermute | solution.py:16
  160.4 7.9 %collective-permute-start = (bf16[2,128,512]{1,2,0:T(8,128)(2,1)}, bf16[2,128,512]{1,2,0:T(8,128)(2,1)S(1)}, u32[]{:S(2)}, u32[]{:S(2)}) collective-permute-start(bf16[2,128,512]{1,2,0:T(8,128)(2,1)} %get-tuple-element.391), channel_id=1, source_target_pairs={{0,1},{1,2},{2,3},{3,4},{4,5},{5,6},{6,7},{7,8},{8,9},{9,10},{10,1... | collective-permute-start | bytes 786440 | tf_op jit(solution)/shard_map/while/body/eval_jaxpr/ppermute | solution.py:16
  176.3 7.9 %collective-permute-start = (bf16[2,128,512]{1,2,0:T(8,128)(2,1)}, bf16[2,128,512]{1,2,0:T(8,128)(2,1)S(1)}, u32[]{:S(2)}, u32[]{:S(2)}) collective-permute-start(bf16[2,128,512]{1,2,0:T(8,128)(2,1)} %get-tuple-element.391), channel_id=1, source_target_pairs={{0,1},{1,2},{2,3},{3,4},{4,5},{5,6},{6,7},{7,8},{8,9},{9,10},{10,1... | collective-permute-start | bytes 786440 | tf_op jit(solution)/shard_map/while/body/eval_jaxpr/ppermute | solution.py:16
  192.2 7.9 %collective-permute-start = (bf16[2,128,512]{1,2,0:T(8,128)(2,1)}, bf16[2,128,512]{1,2,0:T(8,128)(2,1)S(1)}, u32[]{:S(2)}, u32[]{:S(2)}) collective-permute-start(bf16[2,128,512]{1,2,0:T(8,128)(2,1)} %get-tuple-element.391), channel_id=1, source_target_pairs={{0,1},{1,2},{2,3},{3,4},{4,5},{5,6},{6,7},{7,8},{8,9},{9,10},{10,1... | collective-permute-start | bytes 786440 | tf_op jit(solution)/shard_map/while/body/eval_jaxpr/ppermute | solution.py:16
  208.2 7.9 %collective-permute-start = (bf16[2,128,512]{1,2,0:T(8,128)(2,1)}, bf16[2,128,512]{1,2,0:T(8,128)(2,1)S(1)}, u32[]{:S(2)}, u32[]{:S(2)}) collective-permute-start(bf16[2,128,512]{1,2,0:T(8,128)(2,1)} %get-tuple-element.391), channel_id=1, source_target_pairs={{0,1},{1,2},{2,3},{3,4},{4,5},{5,6},{6,7},{7,8},{8,9},{9,10},{10,1... | collective-permute-start | bytes 786440 | tf_op jit(solution)/shard_map/while/body/eval_jaxpr/ppermute | solution.py:16
  224.1 7.9 %collective-permute-start = (bf16[2,128,512]{1,2,0:T(8,128)(2,1)}, bf16[2,128,512]{1,2,0:T(8,128)(2,1)S(1)}, u32[]{:S(2)}, u32[]{:S(2)}) collective-permute-start(bf16[2,128,512]{1,2,0:T(8,128)(2,1)} %get-tuple-element.391), channel_id=1, source_target_pairs={{0,1},{1,2},{2,3},{3,4},{4,5},{5,6},{6,7},{7,8},{8,9},{9,10},{10,1... | collective-permute-start | bytes 786440 | tf_op jit(solution)/shard_map/while/body/eval_jaxpr/ppermute | solution.py:16
  240.0 8.5 %collective-permute-start = (bf16[2,128,512]{1,2,0:T(8,128)(2,1)}, bf16[2,128,512]{1,2,0:T(8,128)(2,1)S(1)}, u32[]{:S(2)}, u32[]{:S(2)}) collective-permute-start(bf16[2,128,512]{1,2,0:T(8,128)(2,1)} %get-tuple-element.391), channel_id=1, source_target_pairs={{0,1},{1,2},{2,3},{3,4},{4,5},{5,6},{6,7},{7,8},{8,9},{9,10},{10,1... | collective-permute-start | bytes 786440 | tf_op jit(solution)/shard_map/while/body/eval_jaxpr/ppermute | solution.py:16
  256.6 10.0 %collective-permute-start = (bf16[2,128,512]{1,2,0:T(8,128)(2,1)}, bf16[2,128,512]{1,2,0:T(8,128)(2,1)S(1)}, u32[]{:S(2)}, u32[]{:S(2)}) collective-permute-start(bf16[2,128,512]{1,2,0:T(8,128)(2,1)} %get-tuple-element.391), channel_id=1, source_target_pairs={{0,1},{1,2},{2,3},{3,4},{4,5},{5,6},{6,7},{7,8},{8,9},{9,10},{10,1... | collective-permute-start | bytes 786440 | tf_op jit(solution)/shard_map/while/body/eval_jaxpr/ppermute | solution.py:16
  353.6 119.4 %copy-start.3 = (bf16[128,4096]{1,0:T(8,128)(2,1)S(1)}, bf16[128,4096]{1,0:T(8,128)(2,1)}, u32[]{:S(2)}) copy-start(bf16[128,4096]{1,0:T(8,128)(2,1)} %param.12) | copy-start | bytes 3145732
  353.6 121.1 %copy-start.6 = (f32[4096]{0:T(1024)S(1)}, f32[4096]{0:T(1024)}, u32[]{:S(2)}) copy-start(f32[4096]{0:T(1024)} %param.18) | copy-start | bytes 49156
  353.6 230.6 %all-gather.2.cloned.1.call-start = ((), (), s32[]{:S(2)}) async-start(), calls=%async_computation.4 | async-start | bytes 9437184 | tf_op jit(solution)/shard_map/all_gather | solution.py:142
  477.3 261.0 %reduce-scatter.5.cloned.1.call-start = ((), (), s32[]{:S(2)}) async-start(), calls=%async_computation.5 | async-start | bytes 9437184 | tf_op jit(solution)/shard_map/reduce_scatter | solution.py:147
  625.5 115.7 %copy-start.1 = (bf16[256,4096]{1,0:T(8,128)(2,1)S(1)}, bf16[256,4096]{1,0:T(8,128)(2,1)}, u32[]{:S(2)}) copy-start(bf16[256,4096]{1,0:T(8,128)(2,1)} %param.17) | copy-start | bytes 6291460
  (2 other events, 2.6 us)
Sparse Core Ops, SparseCore 0:
  353.8 119.2 reduce-scatter.2
  477.4 106.7 all-gather.1
  625.7 112.5 reduce-scatter.4
where the time goes:
time: 750 us; the launch traced here: 748 us
  waiting for transfers between devices  393 us (52%)
  matrix products  96.2 us (13%)
  local copies, waits for them, and re-layouts  83.5 us (11%)
  starting transfers between devices  71.7 us (10%)
  blocking collectives  70.7 us (9%)
  other arithmetic  18.2 us (2%)
  between operations  13.3 us (2%)
    reduce_scatter x1, waiting for transfers between devices, per_device(): lax.psum_scatter(jnp.dot(spread, w_out, preferred_element_type=jnp.float3...  119 us
    reduce_scatter x1, waiting for transfers between devices, per_device(): lax.psum_scatter(partial_rows.astype(jnp.bfloat16), 'dp', scatter_dimensi...  113 us
    all_gather x1, waiting for transfers between devices, per_device(): piece_rows = lax.all_gather(normed, 'dp', axis=0, tiled=True)  107 us
    ppermute x16, starting transfers between devices, from_behind(): return lax.ppermute(block, axis, route)  71.4 us
    all_to_all x1, blocking collectives, per_device(): lax.all_to_all(heads_out, 'dp', split_axis=1, concat_axis=0, tiled=True)  70.7 us
    ppermute x16, waiting for transfers between devices, from_behind(): return lax.ppermute(block, axis, route)  54 us
    dot_general x1, matrix products, per_device(): jnp.dot(hidden_act, w_down, preferred_element_type=jnp.float32)  26.7 us
    squeeze x16, local copies, waits for them, and re-layouts, online_update(): value_rows.reshape(value_rows.shape[0], kv_heads, head_dim)  26.7 us
  transfers between devices with their start and end apart: 19, of which 19 were waited for; matrix products, arithmetic and copies ran while one was open for 0% of the time, Pallas kernels for 0%

commit v1 on v0

--- a/solution.py
+++ b/solution.py
@@ -129,7 +129,10 @@
     heads_out = (
         heads_out.transpose(2, 0, 1, 3).reshape(tok_rows, num_heads * head_dim).astype(jnp.bfloat16)
     )
-    spread = lax.all_to_all(heads_out, "dp", split_axis=1, concat_axis=0, tiled=True)
+    spread = jnp.concatenate(
+        lax.all_to_all(jnp.stack(jnp.split(heads_out, lax.axis_size("dp"), axis=1)), "dp", 0, 0),
+        axis=0,
+    )
     projected = lax.psum_scatter(
         jnp.dot(spread, w_out, preferred_element_type=jnp.float32).astype(jnp.bfloat16),
         "dp",

time: 750 us -> 750 us (level)
  no operation moved by 1% of the time
where the time goes in v1:
time: 750 us; the launch traced here: 748 us
  waiting for transfers between devices  393 us (52%)
  matrix products  96.2 us (13%)
  local copies, waits for them, and re-layouts  83.7 us (11%)
  starting transfers between devices  71.7 us (10%)
  blocking collectives  70.7 us (9%)
  other arithmetic  18.2 us (2%)
  between operations  13.4 us (2%)
    reduce_scatter x1, waiting for transfers between devices, per_device(): lax.psum_scatter(jnp.dot(spread, w_out, preferred_element_type=jnp.float3...  119 us
    reduce_scatter x1, waiting for transfers between devices, per_device(): lax.psum_scatter(partial_rows.astype(jnp.bfloat16), 'dp', scatter_dimensi...  113 us
    all_gather x1, waiting for transfers between devices, per_device(): piece_rows = lax.all_gather(normed, 'dp', axis=0, tiled=True)  107 us
    ppermute x16, starting transfers between devices, from_behind(): return lax.ppermute(block, axis, route)  71.4 us
    all_to_all x1, blocking collectives, per_device(): lax.all_to_all(jnp.stack(jnp.split(heads_out, lax.axis_size('dp'), axis=1...  70.7 us
    ppermute x16, waiting for transfers between devices, from_behind(): return lax.ppermute(block, axis, route)  54 us
    dot_general x1, matrix products, per_device(): jnp.dot(hidden_act, w_down, preferred_element_type=jnp.float32)  26.7 us
    squeeze x16, local copies, waits for them, and re-layouts, online_update(): value_rows.reshape(value_rows.shape[0], kv_heads, head_dim)  26.7 us
  transfers between devices with their start and end apart: 19, of which 19 were waited for; matrix products, arithmetic and copies ran while one was open for 0% of the time, Pallas kernels for 0%

profile of v1, /device:TPU:1, one launch (start us, length us, event | category | flops | bytes accessed | tf_op | source)
XLA Modules:
  0.0 748.2 jit_solution(8058963935906549876)
XLA Ops:
  16.7 258.0 %while.22 = (s32[]{:T(128)}, f32[4,512]{1,0:T(4,128)S(1)}, f32[4,512]{1,0:T(4,128)S(1)}, f32[4,512,128]{2,1,0:T(8,128)S(1)}, bf16[2,128,512]{1,2,0:T(8,128)(2,1)...) while((s32[]{:T(128)}, f32[4,512]{1,0:T(4,128)S(1)}, ...), condition=%wide.region_7.8_spmd.clone, body=%wide.region_4.7_spmd.clone.sunk | while | flops 137154816 | bytes 9210569 | solution.py:126
  16.7 4.6 collective-permute-start
  32.9 4.3 collective-permute-start
  48.8 4.3 collective-permute-start
  64.8 4.3 collective-permute-start
  80.7 4.3 collective-permute-start
  96.6 4.3 collective-permute-start
  112.6 4.3 collective-permute-start
  128.5 4.3 collective-permute-start
  144.4 4.3 collective-permute-start
  160.4 4.3 collective-permute-start
  176.3 4.3 collective-permute-start
  192.2 4.3 collective-permute-start
  208.2 4.3 collective-permute-start
  224.1 4.3 collective-permute-start
  240.0 4.9 collective-permute-start
  256.6 6.4 collective-permute-start
  277.2 70.7 %all_to_all.5 = bf16[8,128,256]{1,2,0:T(8,128)(2,1)S(1)} all-to-all(bf16[8,128,256]{1,2,0:T(8,128)(2,1)S(1)} %fusion.24), channel_id=1, replica_groups=mesh['dp'=8,'ctx'=16] {'dp'}, dimensions={0} | all-to-all | bytes 1048576 | tf_op jit(solution)/shard_map/all_to_all | solution.py:133
  348.2 5.6 convolution_convert_fusion.1
  353.8 119.4 %reduce-scatter.3.cloned.1.call-done = bf16[128,4096]{1,0:T(8,128)(2,1)} async-done(((bf16[1024,4096]{1,0:T(8,128)(2,1)}), bf16[128,4096]{1,0:T(8,128)(2,1)}) %reduce-scatter.3.cloned.1.call-update) | async-done | bytes 1048592 | tf_op jit(solution)/shard_map/reduce_scatter | solution.py:136
  477.7 106.7 %all-gather.2.cloned.1.call-done = bf16[1024,4096]{1,0:T(8,128)(2,1)} async-done(((bf16[128,4096]{1,0:T(8,128)(2,1)}), bf16[1024,4096]{1,0:T(8,128)(2,1)}) %all-gather.2.cloned.1.call-update) | async-done | bytes 8388624 | tf_op jit(solution)/shard_map/all_gather | solution.py:145
  584.4 14.6 %fusion.39 = f32[1024,896]{1,0:T(8,128)} fusion(bf16[1024,4096]{1,0:T(8,128)(2,1)} %all-gather.2.cloned.1.call-done, bf16[4096,896]{1,0:T(8,128)(2,1)} %param.19), kind=kOutput, calls=%fused_computation.83 | convolution fusion | flops 7516192768 | bytes 19398656 | tf_op jit(solution)/shard_map/dot_general | solution.py:146
  599.0 26.7 %convolution_convert_fusion = bf16[1024,4096]{1,0:T(8,128)(2,1)} fusion(bf16[896,4096]{1,0:T(8,128)(2,1)} %param.21, f32[1024,896]{1,0:T(8,128)} %fusion.39, bf16[1024,4096]{1,0:T(8,128)(2,1)} %all-gather.2.cloned.1.call-done, bf16[4096,896]{1,0:T(8,128)(2,1)} %param.20), kind=kOutput, calls=%fused_computation.20 | convolution fusion | flops 15042084864 | bytes 35127296 | tf_op jit(solution)/shard_map/dot_general | solution.py:149
  625.8 112.9 %reduce-scatter.5.cloned.1.call-done = bf16[128,4096]{1,0:T(8,128)(2,1)} async-done(((bf16[1024,4096]{1,0:T(8,128)(2,1)}), bf16[128,4096]{1,0:T(8,128)(2,1)}) %reduce-scatter.5.cloned.1.call-update) | async-done | bytes 1048592 | tf_op jit(solution)/shard_map/reduce_scatter | solution.py:150
  (322 shorter events, 205.5 us)
Async XLA Ops:
  6.5 341.6 %copy-start = (bf16[256,4096]{1,0:T(8,128)(2,1)S(1)}, bf16[256,4096]{1,0:T(8,128)(2,1)}, u32[]{:S(2)}) copy-start(bf16[256,4096]{1,0:T(8,128)(2,1)} %param.17) | copy-start | bytes 6291460
  6.5 466.7 %reduce-scatter.3.cloned.1.call-start = ((), (), s32[]{:S(2)}) async-start(), calls=%async_computation.3 | async-start | bytes 9437184 | tf_op jit(solution)/shard_map/reduce_scatter | solution.py:136
  14.1 1.8 copy-start.5
  16.7 8.2 %collective-permute-start = (bf16[2,128,512]{1,2,0:T(8,128)(2,1)}, bf16[2,128,512]{1,2,0:T(8,128)(2,1)S(1)}, u32[]{:S(2)}, u32[]{:S(2)}) collective-permute-start(bf16[2,128,512]{1,2,0:T(8,128)(2,1)} %get-tuple-element.391), channel_id=1, source_target_pairs={{0,1},{1,2},{2,3},{3,4},{4,5},{5,6},{6,7},{7,8},{8,9},{9,10},{10,1... | collective-permute-start | bytes 786440 | tf_op jit(solution)/shard_map/while/body/eval_jaxpr/ppermute | solution.py:16
  32.9 7.9 %collective-permute-start = (bf16[2,128,512]{1,2,0:T(8,128)(2,1)}, bf16[2,128,512]{1,2,0:T(8,128)(2,1)S(1)}, u32[]{:S(2)}, u32[]{:S(2)}) collective-permute-start(bf16[2,128,512]{1,2,0:T(8,128)(2,1)} %get-tuple-element.391), channel_id=1, source_target_pairs={{0,1},{1,2},{2,3},{3,4},{4,5},{5,6},{6,7},{7,8},{8,9},{9,10},{10,1... | collective-permute-start | bytes 786440 | tf_op jit(solution)/shard_map/while/body/eval_jaxpr/ppermute | solution.py:16
  48.8 7.9 %collective-permute-start = (bf16[2,128,512]{1,2,0:T(8,128)(2,1)}, bf16[2,128,512]{1,2,0:T(8,128)(2,1)S(1)}, u32[]{:S(2)}, u32[]{:S(2)}) collective-permute-start(bf16[2,128,512]{1,2,0:T(8,128)(2,1)} %get-tuple-element.391), channel_id=1, source_target_pairs={{0,1},{1,2},{2,3},{3,4},{4,5},{5,6},{6,7},{7,8},{8,9},{9,10},{10,1... | collective-permute-start | bytes 786440 | tf_op jit(solution)/shard_map/while/body/eval_jaxpr/ppermute | solution.py:16
  64.8 7.9 %collective-permute-start = (bf16[2,128,512]{1,2,0:T(8,128)(2,1)}, bf16[2,128,512]{1,2,0:T(8,128)(2,1)S(1)}, u32[]{:S(2)}, u32[]{:S(2)}) collective-permute-start(bf16[2,128,512]{1,2,0:T(8,128)(2,1)} %get-tuple-element.391), channel_id=1, source_target_pairs={{0,1},{1,2},{2,3},{3,4},{4,5},{5,6},{6,7},{7,8},{8,9},{9,10},{10,1... | collective-permute-start | bytes 786440 | tf_op jit(solution)/shard_map/while/body/eval_jaxpr/ppermute | solution.py:16
  80.7 7.9 %collective-permute-start = (bf16[2,128,512]{1,2,0:T(8,128)(2,1)}, bf16[2,128,512]{1,2,0:T(8,128)(2,1)S(1)}, u32[]{:S(2)}, u32[]{:S(2)}) collective-permute-start(bf16[2,128,512]{1,2,0:T(8,128)(2,1)} %get-tuple-element.391), channel_id=1, source_target_pairs={{0,1},{1,2},{2,3},{3,4},{4,5},{5,6},{6,7},{7,8},{8,9},{9,10},{10,1... | collective-permute-start | bytes 786440 | tf_op jit(solution)/shard_map/while/body/eval_jaxpr/ppermute | solution.py:16
  96.6 7.9 %collective-permute-start = (bf16[2,128,512]{1,2,0:T(8,128)(2,1)}, bf16[2,128,512]{1,2,0:T(8,128)(2,1)S(1)}, u32[]{:S(2)}, u32[]{:S(2)}) collective-permute-start(bf16[2,128,512]{1,2,0:T(8,128)(2,1)} %get-tuple-element.391), channel_id=1, source_target_pairs={{0,1},{1,2},{2,3},{3,4},{4,5},{5,6},{6,7},{7,8},{8,9},{9,10},{10,1... | collective-permute-start | bytes 786440 | tf_op jit(solution)/shard_map/while/body/eval_jaxpr/ppermute | solution.py:16
  112.6 7.9 %collective-permute-start = (bf16[2,128,512]{1,2,0:T(8,128)(2,1)}, bf16[2,128,512]{1,2,0:T(8,128)(2,1)S(1)}, u32[]{:S(2)}, u32[]{:S(2)}) collective-permute-start(bf16[2,128,512]{1,2,0:T(8,128)(2,1)} %get-tuple-element.391), channel_id=1, source_target_pairs={{0,1},{1,2},{2,3},{3,4},{4,5},{5,6},{6,7},{7,8},{8,9},{9,10},{10,1... | collective-permute-start | bytes 786440 | tf_op jit(solution)/shard_map/while/body/eval_jaxpr/ppermute | solution.py:16
  128.5 7.9 %collective-permute-start = (bf16[2,128,512]{1,2,0:T(8,128)(2,1)}, bf16[2,128,512]{1,2,0:T(8,128)(2,1)S(1)}, u32[]{:S(2)}, u32[]{:S(2)}) collective-permute-start(bf16[2,128,512]{1,2,0:T(8,128)(2,1)} %get-tuple-element.391), channel_id=1, source_target_pairs={{0,1},{1,2},{2,3},{3,4},{4,5},{5,6},{6,7},{7,8},{8,9},{9,10},{10,1... | collective-permute-start | bytes 786440 | tf_op jit(solution)/shard_map/while/body/eval_jaxpr/ppermute | solution.py:16
  144.4 7.9 %collective-permute-start = (bf16[2,128,512]{1,2,0:T(8,128)(2,1)}, bf16[2,128,512]{1,2,0:T(8,128)(2,1)S(1)}, u32[]{:S(2)}, u32[]{:S(2)}) collective-permute-start(bf16[2,128,512]{1,2,0:T(8,128)(2,1)} %get-tuple-element.391), channel_id=1, source_target_pairs={{0,1},{1,2},{2,3},{3,4},{4,5},{5,6},{6,7},{7,8},{8,9},{9,10},{10,1... | collective-permute-start | bytes 786440 | tf_op jit(solution)/shard_map/while/body/eval_jaxpr/ppermute | solution.py:16
  160.4 7.9 %collective-permute-start = (bf16[2,128,512]{1,2,0:T(8,128)(2,1)}, bf16[2,128,512]{1,2,0:T(8,128)(2,1)S(1)}, u32[]{:S(2)}, u32[]{:S(2)}) collective-permute-start(bf16[2,128,512]{1,2,0:T(8,128)(2,1)} %get-tuple-element.391), channel_id=1, source_target_pairs={{0,1},{1,2},{2,3},{3,4},{4,5},{5,6},{6,7},{7,8},{8,9},{9,10},{10,1... | collective-permute-start | bytes 786440 | tf_op jit(solution)/shard_map/while/body/eval_jaxpr/ppermute | solution.py:16
  176.3 7.9 %collective-permute-start = (bf16[2,128,512]{1,2,0:T(8,128)(2,1)}, bf16[2,128,512]{1,2,0:T(8,128)(2,1)S(1)}, u32[]{:S(2)}, u32[]{:S(2)}) collective-permute-start(bf16[2,128,512]{1,2,0:T(8,128)(2,1)} %get-tuple-element.391), channel_id=1, source_target_pairs={{0,1},{1,2},{2,3},{3,4},{4,5},{5,6},{6,7},{7,8},{8,9},{9,10},{10,1... | collective-permute-start | bytes 786440 | tf_op jit(solution)/shard_map/while/body/eval_jaxpr/ppermute | solution.py:16
  192.2 7.9 %collective-permute-start = (bf16[2,128,512]{1,2,0:T(8,128)(2,1)}, bf16[2,128,512]{1,2,0:T(8,128)(2,1)S(1)}, u32[]{:S(2)}, u32[]{:S(2)}) collective-permute-start(bf16[2,128,512]{1,2,0:T(8,128)(2,1)} %get-tuple-element.391), channel_id=1, source_target_pairs={{0,1},{1,2},{2,3},{3,4},{4,5},{5,6},{6,7},{7,8},{8,9},{9,10},{10,1... | collective-permute-start | bytes 786440 | tf_op jit(solution)/shard_map/while/body/eval_jaxpr/ppermute | solution.py:16
  208.2 7.9 %collective-permute-start = (bf16[2,128,512]{1,2,0:T(8,128)(2,1)}, bf16[2,128,512]{1,2,0:T(8,128)(2,1)S(1)}, u32[]{:S(2)}, u32[]{:S(2)}) collective-permute-start(bf16[2,128,512]{1,2,0:T(8,128)(2,1)} %get-tuple-element.391), channel_id=1, source_target_pairs={{0,1},{1,2},{2,3},{3,4},{4,5},{5,6},{6,7},{7,8},{8,9},{9,10},{10,1... | collective-permute-start | bytes 786440 | tf_op jit(solution)/shard_map/while/body/eval_jaxpr/ppermute | solution.py:16
  224.1 7.9 %collective-permute-start = (bf16[2,128,512]{1,2,0:T(8,128)(2,1)}, bf16[2,128,512]{1,2,0:T(8,128)(2,1)S(1)}, u32[]{:S(2)}, u32[]{:S(2)}) collective-permute-start(bf16[2,128,512]{1,2,0:T(8,128)(2,1)} %get-tuple-element.391), channel_id=1, source_target_pairs={{0,1},{1,2},{2,3},{3,4},{4,5},{5,6},{6,7},{7,8},{8,9},{9,10},{10,1... | collective-permute-start | bytes 786440 | tf_op jit(solution)/shard_map/while/body/eval_jaxpr/ppermute | solution.py:16
  240.0 8.5 %collective-permute-start = (bf16[2,128,512]{1,2,0:T(8,128)(2,1)}, bf16[2,128,512]{1,2,0:T(8,128)(2,1)S(1)}, u32[]{:S(2)}, u32[]{:S(2)}) collective-permute-start(bf16[2,128,512]{1,2,0:T(8,128)(2,1)} %get-tuple-element.391), channel_id=1, source_target_pairs={{0,1},{1,2},{2,3},{3,4},{4,5},{5,6},{6,7},{7,8},{8,9},{9,10},{10,1... | collective-permute-start | bytes 786440 | tf_op jit(solution)/shard_map/while/body/eval_jaxpr/ppermute | solution.py:16
  256.6 10.0 %collective-permute-start = (bf16[2,128,512]{1,2,0:T(8,128)(2,1)}, bf16[2,128,512]{1,2,0:T(8,128)(2,1)S(1)}, u32[]{:S(2)}, u32[]{:S(2)}) collective-permute-start(bf16[2,128,512]{1,2,0:T(8,128)(2,1)} %get-tuple-element.391), channel_id=1, source_target_pairs={{0,1},{1,2},{2,3},{3,4},{4,5},{5,6},{6,7},{7,8},{8,9},{9,10},{10,1... | collective-permute-start | bytes 786440 | tf_op jit(solution)/shard_map/while/body/eval_jaxpr/ppermute | solution.py:16
  353.8 119.5 %copy-start.3 = (bf16[128,4096]{1,0:T(8,128)(2,1)S(1)}, bf16[128,4096]{1,0:T(8,128)(2,1)}, u32[]{:S(2)}) copy-start(bf16[128,4096]{1,0:T(8,128)(2,1)} %param.12) | copy-start | bytes 3145732
  353.8 121.1 %copy-start.6 = (f32[4096]{0:T(1024)S(1)}, f32[4096]{0:T(1024)}, u32[]{:S(2)}) copy-start(f32[4096]{0:T(1024)} %param.18) | copy-start | bytes 49156
  353.8 230.7 %all-gather.2.cloned.1.call-start = ((), (), s32[]{:S(2)}) async-start(), calls=%async_computation.4 | async-start | bytes 9437184 | tf_op jit(solution)/shard_map/all_gather | solution.py:145
  477.5 261.2 %reduce-scatter.5.cloned.1.call-start = ((), (), s32[]{:S(2)}) async-start(), calls=%async_computation.5 | async-start | bytes 9437184 | tf_op jit(solution)/shard_map/reduce_scatter | solution.py:150
  625.7 115.9 %copy-start.1 = (bf16[256,4096]{1,0:T(8,128)(2,1)S(1)}, bf16[256,4096]{1,0:T(8,128)(2,1)}, u32[]{:S(2)}) copy-start(bf16[256,4096]{1,0:T(8,128)(2,1)} %param.17) | copy-start | bytes 6291460
  (2 other events, 2.6 us)
Sparse Core Ops, SparseCore 0:
  353.9 119.2 reduce-scatter.2
  477.6 106.7 all-gather.1
  625.9 112.7 reduce-scatter.4
